TPU v7x, 512 devices: a whole 4x4x16 slice. The times are simulated.
512 devices in a mesh: sub: 128 (over z, x, core), tile: 4 (over y).
Axes of the slice: x: 4, y: 4, z: 16, core: 2. Of those that a mesh axis runs over, the one named last changes fastest.
Arguments:
- ray_cot: float32 [4, 4, 32768], P(None, 'tile', 'sub'), may hold values from -6 to 6
- ray_lists: int32 [4, 32768, 8], P('tile', 'sub'), may hold values from 0 to 127, all different within a row; in each aligned block of 256 rows (0 to 255, 256 to 511, ..., all dimensions but the last counted through in order) at most 32 rows name the same one
- geometry: float32 [7, 262144], P(None, 'sub'), may hold values from -1024 to 1024, as said below
- sh_coef: float32 [48, 262144], P(None, 'sub'), may hold values from -1.8 to 1.8
- view_angles: float32 [4, 2], replicated, may hold values from -3.140625 to 3.140625
- block_ids: int32 [128, 4, 4], P('sub', 'tile'), may hold values from 0 to 15, as said below
- block_counts: int32 [128, 4], P('sub', 'tile'), may hold values from 1 to 4, as said below
Outputs:
- geo_grad: float32 [7, 262144], P(None, 'sub')
- sh_grad: float32 [48, 262144], P(None, 'sub')
Inputs may be any that keep to these rules, and one draw needn't show every extreme that they name: `ray_lists`: each row names 8 different subspaces, in the order in which the ray meets them; among the rows of one device no subspace is named more than 32 times, a bound that some block reaches. `block_ids`: each list holds 4 different resident block numbers. `block_counts`: both ends are reached in every draw. `geometry`: rows 0 and 1 are a Gaussian's centre in pixels (column, row); rows 2 to 4 are A, B, C of a positive definite inverse covariance [[A, B], [B, C]]; row 5 is an opacity between 0.05 and 0.9; row 6 is a depth between 0.5 and 2.
All inputs are finite; a program needn't handle non-finite values.
Results may differ from a plain program's by a relative error of at most 0.0003.
Values sent between devices are 32-bit elements; how exact they have to be, the bound alone decides.
A program may use at most 64 MiB of HBM per device.

v0:
```python
import jax
import jax.numpy as jnp
from jax import lax
from jax.sharding import PartitionSpec as P

IMG_W = 1024
BLOCK = 128


distant = -10000.0
highest = lax.Precision.HIGHEST


def view_basis(angle_pair):
    azimuth = angle_pair[0]
    elevation = angle_pair[1]
    along_x = jnp.cos(elevation) * jnp.cos(azimuth)
    along_y = jnp.cos(elevation) * jnp.sin(azimuth)
    along_z = jnp.sin(elevation)
    square_x = along_x * along_x
    square_y = along_y * along_y
    square_z = along_z * along_z
    terms = [
        0.28209479177387814 * jnp.ones_like(along_x),
        -0.4886025119029199 * along_y,
        0.4886025119029199 * along_z,
        -0.4886025119029199 * along_x,
        1.0925484305920792 * along_x * along_y,
        -1.0925484305920792 * along_y * along_z,
        0.31539156525252005 * (2.0 * square_z - square_x - square_y),
        -1.0925484305920792 * along_x * along_z,
        0.5462742152960396 * (square_x - square_y),
        -0.5900435899266435 * along_y * (3.0 * square_x - square_y),
        2.890611442640554 * along_x * along_y * along_z,
        -0.4570457994644658 * along_y * (4.0 * square_z - square_x - square_y),
        0.3731763325901154 * along_z * (2.0 * square_z - 3.0 * square_x - 3.0 * square_y),
        -0.4570457994644658 * along_x * (4.0 * square_z - square_x - square_y),
        1.445305721320277 * along_z * (square_x - square_y),
        -0.5900435899266435 * along_x * (square_x - 3.0 * square_y),
    ]
    return jnp.stack(terms)


def colours(sh_coef, harmonics):
    table = sh_coef.reshape(16, 3, -1)
    return 0.5 + jnp.einsum("k,kcg->cg", harmonics, table, precision=highest)


def render(block_geometry, block_features, block_active, coords):
    slot_count = coords.shape[1]
    block_size = block_geometry.shape[2]
    lower = (
        jnp.arange(block_size, dtype=jnp.int32)[:, None]
        > jnp.arange(block_size, dtype=jnp.int32)[None, :]
    ).astype(jnp.float32)

    def advance(running, inputs):
        gathered, passing = running
        shapes, tinted, active = inputs
        offset_x = coords[0][None, :] - shapes[0][:, None]
        offset_y = coords[1][None, :] - shapes[1][:, None]
        exponent = (
            shapes[2][:, None] * offset_x * offset_x
            + 2.0 * shapes[3][:, None] * offset_x * offset_y
            + shapes[4][:, None] * offset_y * offset_y
        )
        alphas = active * shapes[5][:, None] * jnp.exp(-0.5 * exponent)
        log_keep = jnp.log1p(-alphas)
        before = jnp.dot(lower, log_keep, precision=highest)
        weights = alphas * passing[None, :] * jnp.exp(before)
        gathered = gathered + jnp.dot(tinted, weights, precision=highest)
        passing = passing * jnp.exp(jnp.sum(log_keep, axis=0))
        return ((gathered, passing), None)

    initial = (jnp.zeros((4, slot_count), jnp.float32), jnp.ones((slot_count,), jnp.float32))
    scanned = (
        jnp.transpose(block_geometry, (1, 0, 2)),
        jnp.transpose(block_features, (1, 0, 2)),
        block_active,
    )
    (gathered, passing), _ = lax.scan(jax.checkpoint(advance), initial, scanned)
    return jnp.concatenate([gathered, passing[None, :]], axis=0)


def compose(entries):
    result = jnp.zeros_like(entries[:4, :, 0])
    carried = jnp.ones_like(entries[4, :, 0])
    for column in range(entries.shape[2]):
        result = result + carried[None, :] * entries[:4, :, column]
        carried = carried * entries[4, :, column]
    return result


def body(ray_cot, ray_lists, geometry, sh_coef, view_angles, block_ids, block_counts):
    sub_count = lax.axis_size("sub")
    sub_index = lax.axis_index("sub")
    view_index = lax.axis_index("tile")
    ray_count = ray_lists.shape[1]
    listed = ray_lists.shape[2]
    capacity = ray_count * 16 // sub_count
    targets = ray_lists[0].reshape(-1)
    matches = (targets[:, None] == jnp.arange(sub_count, dtype=jnp.int32)[None, :]).astype(
        jnp.int32
    )
    entry_rank = jnp.sum((jnp.cumsum(matches, axis=0) - matches) * matches, axis=1)
    slot_index = targets * capacity + entry_rank
    ray_index = sub_index * ray_count + jnp.arange(ray_count, dtype=jnp.int32)
    pixels = jnp.stack(
        [(ray_index % IMG_W).astype(jnp.float32), (ray_index // IMG_W).astype(jnp.float32)]
    )
    pixel_entries = jnp.repeat(pixels, listed, axis=1)
    outgoing = (
        jnp.full((2, sub_count * capacity), distant, jnp.float32)
        .at[:, slot_index]
        .set(pixel_entries)
    )
    queries = lax.all_to_all(
        outgoing.reshape(2, sub_count, capacity), "sub", split_axis=1, concat_axis=1, tiled=True
    )
    queries = queries.reshape(2, sub_count * capacity)
    harmonics = view_basis(view_angles[view_index])
    features = jnp.concatenate([colours(sh_coef, harmonics), geometry[6:7]], axis=0)
    resident = geometry.shape[1] // BLOCK
    chosen = block_ids[0, 0]
    picker = (chosen[:, None] == jnp.arange(resident, dtype=jnp.int32)[None, :]).astype(jnp.float32)
    block_geo = jnp.einsum(
        "cbg,lb->clg",
        geometry.reshape(geometry.shape[0], resident, BLOCK),
        picker,
        precision=highest,
    )
    block_feat = jnp.einsum(
        "cbg,lb->clg", features.reshape(4, resident, BLOCK), picker, precision=highest
    )
    active = (jnp.arange(chosen.shape[0], dtype=jnp.int32) < block_counts[0, 0]).astype(jnp.float32)

    def forward(shapes, tinted):
        return render(shapes, tinted, active, queries)

    partials, pullback = jax.vjp(forward, block_geo, block_feat)
    returned = lax.all_to_all(
        partials.reshape(5, sub_count, capacity), "sub", split_axis=1, concat_axis=1, tiled=True
    )
    picked = returned.reshape(5, -1)[:, slot_index].reshape(5, ray_count, listed)
    compose_back = jax.vjp(compose, picked)[1]
    slot_cot = compose_back(ray_cot[:, 0, :])[0]
    outgoing_cot = (
        jnp.zeros((5, sub_count * capacity), jnp.float32)
        .at[:, slot_index]
        .set(slot_cot.reshape(5, -1))
    )
    incoming = lax.all_to_all(
        outgoing_cot.reshape(5, sub_count, capacity), "sub", split_axis=1, concat_axis=1, tiled=True
    )
    geo_block_grad, feat_block_grad = pullback(incoming.reshape(5, -1))
    geo_local = jnp.einsum("clg,lb->cbg", geo_block_grad, picker, precision=highest).reshape(
        geometry.shape[0], -1
    )
    feat_local = jnp.einsum("clg,lb->cbg", feat_block_grad, picker, precision=highest).reshape(
        4, -1
    )
    geo_local = geo_local.at[6].add(feat_local[3])
    colour_grad = feat_local[:3]
    sh_local = (harmonics[:, None, None] * colour_grad[None, :, :]).reshape(sh_coef.shape[0], -1)
    geo_grad, sh_grad = lax.psum((geo_local, sh_local), "tile")
    return (geo_grad, sh_grad)


def solution(mesh):
    return jax.shard_map(
        body,
        mesh=mesh,
        in_specs=(
            P(None, "tile", "sub"),
            P("tile", "sub", None),
            P(None, "sub"),
            P(None, "sub"),
            P(),
            P("sub", "tile", None),
            P("sub", "tile"),
        ),
        out_specs=(P(None, "sub"), P(None, "sub")),
        check_vma=False,
    )
```

profile of v0, /device:TPU:4, one launch (start us, length us, event | category | flops | bytes accessed | tf_op | source)
XLA Modules:
  0.0 305.6 jit_solution(6351711274316427150)
XLA Ops:
  11.0 6.1 %scatter_custom_fusion = f32[2,4096]{0,1:T(8,128)S(1)} fusion(s32[2048]{0:T(1024)S(1)} %bitcast.307, f32[]{:T(128)} %constant.211.clone.1, f32[2,256]{0,1:T(8,128)S(1)} %copy.103), kind=kCustom, calls=%fused_computation.113 | custom fusion | bytes 163844 | tf_op jit(solution)/shard_map/scatter | solution.py:115
  18.6 19.7 %all-to-all-start = ((f32[2,128,32]{2,0,1:T(2,128)}), f32[2,128,32]{2,0,1:T(2,128)S(1)}, u32[]{:S(2)}, u32[]{:S(2)}) async-start(f32[2,128,32]{2,0,1:T(2,128)} %copy.104), calls=%async_computation | async-start | bytes 262144 | tf_op jit(solution)/shard_map/all_to_all | solution.py:117
  44.0 10.2 %all-to-all-done = f32[2,128,32]{2,0,1:T(2,128)S(1)} async-done(((f32[2,128,32]{2,0,1:T(2,128)}), f32[2,128,32]{2,0,1:T(2,128)S(1)}, u32[]{:S(2)}, u32[]{:S(2)}) %all-to-all-start) | async-done | bytes 32800 | tf_op jit(solution)/shard_map/all_to_all | solution.py:117
  54.8 38.8 %while.38 = (s32[]{:T(128)}, f32[4,4096]{1,0:T(4,128)S(1)}, f32[4096]{0:T(1024)S(1)}, f32[4,4096]{1,0:T(4,128)S(1)}, f32[4,4,128]{2,1,0:T(4,128)S(1)}, /*index=5...) while((s32[]{:T(128)}, f32[4,4096]{1,0:T(4,128)S(1)}, ...), condition=%wide.region_6.7_spmd.clone, body=%wide.region_4.6_spmd.clone.sunk | while | flops 852037888 | bytes 4543644 | solution.py:81
  58.7 4.0 %fusion.147 = f32[128,4096]{0,1:T(8,128)S(1)} fusion(f32[4096]{0:T(1024)S(1)} %get-tuple-element.759, f32[128]{0:T(128)S(1)} %get-tuple-element.753, f32[128]{0:T(128)S(1)} %get-tuple-element.754, f32[4096]{0:T(1024)S(1)} %bitcast.317, f32[128]{0:T(128)S(1)} %get-tuple-element.755, f32[128]{0:T(128)S(1)} %get-tuple-element.756, ...), kind=kOutput, calls=%fused_computation.82.clone.1 | convolution fusion | flops 819494912 | bytes 2149376 | tf_op jit(solution)/shard_map/jvp()/while/body/eval_jaxpr/dot_general | solution.py:69
  68.4 4.0 %fusion.147 = f32[128,4096]{0,1:T(8,128)S(1)} fusion(f32[4096]{0:T(1024)S(1)} %get-tuple-element.759, f32[128]{0:T(128)S(1)} %get-tuple-element.753, f32[128]{0:T(128)S(1)} %get-tuple-element.754, f32[4096]{0:T(1024)S(1)} %bitcast.317, f32[128]{0:T(128)S(1)} %get-tuple-element.755, f32[128]{0:T(128)S(1)} %get-tuple-element.756, ...), kind=kOutput, calls=%fused_computation.82.clone.1 | convolution fusion | flops 819494912 | bytes 2149376 | tf_op jit(solution)/shard_map/jvp()/while/body/eval_jaxpr/dot_general | solution.py:69
  78.1 4.0 %fusion.147 = f32[128,4096]{0,1:T(8,128)S(1)} fusion(f32[4096]{0:T(1024)S(1)} %get-tuple-element.759, f32[128]{0:T(128)S(1)} %get-tuple-element.753, f32[128]{0:T(128)S(1)} %get-tuple-element.754, f32[4096]{0:T(1024)S(1)} %bitcast.317, f32[128]{0:T(128)S(1)} %get-tuple-element.755, f32[128]{0:T(128)S(1)} %get-tuple-element.756, ...), kind=kOutput, calls=%fused_computation.82.clone.1 | convolution fusion | flops 819494912 | bytes 2149376 | tf_op jit(solution)/shard_map/jvp()/while/body/eval_jaxpr/dot_general | solution.py:69
  87.8 4.0 %fusion.147 = f32[128,4096]{0,1:T(8,128)S(1)} fusion(f32[4096]{0:T(1024)S(1)} %get-tuple-element.759, f32[128]{0:T(128)S(1)} %get-tuple-element.753, f32[128]{0:T(128)S(1)} %get-tuple-element.754, f32[4096]{0:T(1024)S(1)} %bitcast.317, f32[128]{0:T(128)S(1)} %get-tuple-element.755, f32[128]{0:T(128)S(1)} %get-tuple-element.756, ...), kind=kOutput, calls=%fused_computation.82.clone.1 | convolution fusion | flops 819494912 | bytes 2149376 | tf_op jit(solution)/shard_map/jvp()/while/body/eval_jaxpr/dot_general | solution.py:69
  95.0 7.7 %all-to-all-start.1 = ((f32[128,1,160]{2,1,0:T(1,128)}), f32[128,1,160]{2,1,0:T(1,128)S(1)}, u32[]{:S(2)}, u32[]{:S(2)}) async-start(f32[128,1,160]{2,1,0:T(1,128)} %reshape.864), calls=%async_computation.1 | async-start | bytes 262144 | tf_op jit(solution)/shard_map/all_to_all | solution.py:141
  102.7 15.9 %all-to-all-done.1 = f32[128,1,160]{2,1,0:T(1,128)S(1)} async-done(((f32[128,1,160]{2,1,0:T(1,128)}), f32[128,1,160]{2,1,0:T(1,128)S(1)}, u32[]{:S(2)}, u32[]{:S(2)}) %all-to-all-start.1) | async-done | bytes 81952 | tf_op jit(solution)/shard_map/all_to_all | solution.py:141
  121.2 5.5 %gather_fusion = f32[2048,5]{1,0:T(8,128)S(1)} fusion(f32[5,4096]{0,1:T(8,128)S(1)} %bitcast.274, s32[2048]{0:T(1024)S(1)} %broadcast_clamp_fusion), kind=kCustom, calls=%fused_computation | custom fusion | bytes 90112 | tf_op jit(solution)/shard_map/gather | solution.py:144
  131.7 6.1 %scatter_custom_fusion.1 = f32[5,4096]{0,1:T(8,128)S(1)} fusion(s32[2048]{0:T(1024)S(1)} %bitcast.309, f32[2048,5]{1,0:T(8,128)S(1)} %copy.124, f32[]{:T(128)} %constant.189.clone.1), kind=kCustom, calls=%fused_computation.123 | custom fusion | bytes 81924 | tf_op jit(solution)/shard_map/scatter | solution.py:150
  139.6 7.2 %all-to-all-start.2 = ((f32[128,1,160]{2,1,0:T(1,128)}), f32[128,1,160]{2,1,0:T(1,128)S(1)}, u32[]{:S(2)}, u32[]{:S(2)}) async-start(f32[128,1,160]{2,1,0:T(1,128)} %reshape.866), calls=%async_computation.2 | async-start | bytes 262144 | tf_op jit(solution)/shard_map/all_to_all | solution.py:152
  147.1 15.7 %all-to-all-done.2 = f32[128,1,160]{2,1,0:T(1,128)S(1)} async-done(((f32[128,1,160]{2,1,0:T(1,128)}), f32[128,1,160]{2,1,0:T(1,128)S(1)}, u32[]{:S(2)}, u32[]{:S(2)}) %all-to-all-start.2) | async-done | bytes 81952 | tf_op jit(solution)/shard_map/all_to_all | solution.py:152
  164.4 80.7 %while.37 = (s32[]{:T(128)}, f32[4,4096]{1,0:T(4,128)S(1)}, f32[4096]{0:T(1024)S(1)}, f32[4,7,128]{2,1,0:T(8,128)S(1)}, f32[4,4,128]{2,1,0:T(4,128)S(1)}, /*inde...) while((s32[]{:T(128)}, f32[4,4096]{1,0:T(4,128)S(1)}, ...), condition=%wide.region_24.25_spmd.clone, body=%wide.region_15.24_spmd.clone.sunk | while | flops 1721282944 | bytes 21792424 | solution.py:81
  172.2 4.0 %log-plus-one_reduce_fusion.2 = (f32[4096]{0:T(1024)S(1)}, f32[4096]{0:T(1024)S(1)}, f32[128,4096]{1,0:T(8,128)S(1)}) fusion(f32[128]{0:T(128)S(1)} %get-tuple-element.716, f32[128]{0:T(128)S(1)} %get-tuple-element.717, f32[4096]{0:T(1024)S(1)} %bitcast.285, f32[128]{0:T(128)S(1)} %get-tuple-element.720, f32[128]{0:T(128)S(1)} %get-tuple-element.721, ...), kind=kOutput, calls=%fused_computation.47.clone.1 | convolution fusion | flops 34070528 | bytes 4330496 | tf_op jit(solution)/shard_map/transpose(jvp())/while/body/eval_jaxpr/checkpoint/dot_general | solution.py:71
  176.2 4.8 %multiply_multiply_fusion.11 = (f32[128,4096]{1,0:T(8,128)S(1)}, f32[128,4096]{1,0:T(8,128)S(1)}) fusion(f32[128]{0:T(128)S(1)} %get-tuple-element.716, f32[128]{0:T(128)S(1)} %get-tuple-element.717, f32[4096]{0:T(1024)S(1)} %bitcast.286, f32[128]{0:T(128)S(1)} %get-tuple-element.720, f32[128]{0:T(128)S(1)} %get-tuple-element.721, ...), kind=kOutput, calls=%fused_computation.39.clone.1 | convolution fusion | flops 825229312 | bytes 8522752 | tf_op jit(solution)/shard_map/transpose(jvp())/while/body/eval_jaxpr/checkpoint/dot_general | solution.py:69
  196.4 4.8 %multiply_multiply_fusion.11 = (f32[128,4096]{1,0:T(8,128)S(1)}, f32[128,4096]{1,0:T(8,128)S(1)}) fusion(f32[128]{0:T(128)S(1)} %get-tuple-element.716, f32[128]{0:T(128)S(1)} %get-tuple-element.717, f32[4096]{0:T(1024)S(1)} %bitcast.286, f32[128]{0:T(128)S(1)} %get-tuple-element.720, f32[128]{0:T(128)S(1)} %get-tuple-element.721, ...), kind=kOutput, calls=%fused_computation.39.clone.1 | convolution fusion | flops 825229312 | bytes 8522752 | tf_op jit(solution)/shard_map/transpose(jvp())/while/body/eval_jaxpr/checkpoint/dot_general | solution.py:69
  212.5 4.0 %log-plus-one_reduce_fusion.2 = (f32[4096]{0:T(1024)S(1)}, f32[4096]{0:T(1024)S(1)}, f32[128,4096]{1,0:T(8,128)S(1)}) fusion(f32[128]{0:T(128)S(1)} %get-tuple-element.716, f32[128]{0:T(128)S(1)} %get-tuple-element.717, f32[4096]{0:T(1024)S(1)} %bitcast.285, f32[128]{0:T(128)S(1)} %get-tuple-element.720, f32[128]{0:T(128)S(1)} %get-tuple-element.721, ...), kind=kOutput, calls=%fused_computation.47.clone.1 | convolution fusion | flops 34070528 | bytes 4330496 | tf_op jit(solution)/shard_map/transpose(jvp())/while/body/eval_jaxpr/checkpoint/dot_general | solution.py:71
  216.5 4.8 %multiply_multiply_fusion.11 = (f32[128,4096]{1,0:T(8,128)S(1)}, f32[128,4096]{1,0:T(8,128)S(1)}) fusion(f32[128]{0:T(128)S(1)} %get-tuple-element.716, f32[128]{0:T(128)S(1)} %get-tuple-element.717, f32[4096]{0:T(1024)S(1)} %bitcast.286, f32[128]{0:T(128)S(1)} %get-tuple-element.720, f32[128]{0:T(128)S(1)} %get-tuple-element.721, ...), kind=kOutput, calls=%fused_computation.39.clone.1 | convolution fusion | flops 825229312 | bytes 8522752 | tf_op jit(solution)/shard_map/transpose(jvp())/while/body/eval_jaxpr/checkpoint/dot_general | solution.py:69
  232.6 4.0 %log-plus-one_reduce_fusion.2 = (f32[4096]{0:T(1024)S(1)}, f32[4096]{0:T(1024)S(1)}, f32[128,4096]{1,0:T(8,128)S(1)}) fusion(f32[128]{0:T(128)S(1)} %get-tuple-element.716, f32[128]{0:T(128)S(1)} %get-tuple-element.717, f32[4096]{0:T(1024)S(1)} %bitcast.285, f32[128]{0:T(128)S(1)} %get-tuple-element.720, f32[128]{0:T(128)S(1)} %get-tuple-element.721, ...), kind=kOutput, calls=%fused_computation.47.clone.1 | convolution fusion | flops 34070528 | bytes 4330496 | tf_op jit(solution)/shard_map/transpose(jvp())/while/body/eval_jaxpr/checkpoint/dot_general | solution.py:71
  236.6 4.8 %multiply_multiply_fusion.11 = (f32[128,4096]{1,0:T(8,128)S(1)}, f32[128,4096]{1,0:T(8,128)S(1)}) fusion(f32[128]{0:T(128)S(1)} %get-tuple-element.716, f32[128]{0:T(128)S(1)} %get-tuple-element.717, f32[4096]{0:T(1024)S(1)} %bitcast.286, f32[128]{0:T(128)S(1)} %get-tuple-element.720, f32[128]{0:T(128)S(1)} %get-tuple-element.721, ...), kind=kOutput, calls=%fused_computation.39.clone.1 | convolution fusion | flops 825229312 | bytes 8522752 | tf_op jit(solution)/shard_map/transpose(jvp())/while/body/eval_jaxpr/checkpoint/dot_general | solution.py:69
  247.2 18.6 %psum.14 = f32[7,2048]{1,0:T(8,128)} all-reduce(f32[7,2048]{1,0:T(8,128)S(1)} %scatter-add.4), channel_id=1, replica_groups=mesh['sub'=128,'tile'=4] {'tile'}, use_global_device_ids=true, to_apply=%region_25.26 | all-reduce | flops 14336 | bytes 114688 | tf_op jit(solution)/shard_map/psum | solution.py:165
  265.8 31.0 %all-reduce.23.cloned.1.call-done = f32[48,2048]{1,0:T(8,128)} async-done(((f32[48,2048]{1,0:T(8,128)}), f32[48,2048]{1,0:T(8,128)}) %all-reduce.23.cloned.1.call-update) | async-done | bytes 393232 | tf_op jit(solution)/shard_map/psum | solution.py:165
  (198 shorter events, 95.5 us)
Async XLA Ops:
  7.2 31.2 %copy-start = (f32[4,2]{0,1:T(2,128)S(1)}, f32[4,2]{0,1:T(2,128)}, u32[]{:S(2)}) copy-start(f32[4,2]{0,1:T(2,128)} %param.17) | copy-start | bytes 100
  11.0 31.1 %copy-start.2 = (f32[7,2048]{1,0:T(8,128)S(1)}, f32[7,2048]{1,0:T(8,128)}, u32[]{:S(2)}) copy-start(f32[7,2048]{1,0:T(8,128)} %param.15) | copy-start | bytes 172036
  11.0 31.1 %copy-start.1 = (f32[48,2048]{1,0:T(8,128)S(1)}, f32[48,2048]{1,0:T(8,128)}, u32[]{:S(2)}) copy-start(f32[48,2048]{1,0:T(8,128)} %param.16) | copy-start | bytes 1179652
  17.1 25.8 %copy-start.4 = (s32[1,1,4]{2,1,0:T(1,128)S(1)}, s32[1,1,4]{2,1,0:T(1,128)}, u32[]{:S(2)}) copy-start(s32[1,1,4]{2,1,0:T(1,128)} %param.18) | copy-start | bytes 52
  18.6 35.6 %all-to-all-start = ((f32[2,128,32]{2,0,1:T(2,128)}), f32[2,128,32]{2,0,1:T(2,128)S(1)}, u32[]{:S(2)}, u32[]{:S(2)}) async-start(f32[2,128,32]{2,0,1:T(2,128)} %copy.104), calls=%async_computation | async-start | bytes 262144 | tf_op jit(solution)/shard_map/all_to_all | solution.py:117
  95.0 23.6 %all-to-all-start.1 = ((f32[128,1,160]{2,1,0:T(1,128)}), f32[128,1,160]{2,1,0:T(1,128)S(1)}, u32[]{:S(2)}, u32[]{:S(2)}) async-start(f32[128,1,160]{2,1,0:T(1,128)} %reshape.864), calls=%async_computation.1 | async-start | bytes 262144 | tf_op jit(solution)/shard_map/all_to_all | solution.py:141
  128.6 1.9 copy-start.3
  139.6 23.2 %all-to-all-start.2 = ((f32[128,1,160]{2,1,0:T(1,128)}), f32[128,1,160]{2,1,0:T(1,128)S(1)}, u32[]{:S(2)}, u32[]{:S(2)}) async-start(f32[128,1,160]{2,1,0:T(1,128)} %reshape.866), calls=%async_computation.2 | async-start | bytes 262144 | tf_op jit(solution)/shard_map/all_to_all | solution.py:152
  146.7 150.1 %all-reduce.23.cloned.1.call-start = ((), (), s32[]{:S(2)}) async-start(), calls=%async_computation.3 | async-start | bytes 786432 | tf_op jit(solution)/shard_map/psum | solution.py:165
Sparse Core Ops, SparseCore 0:
  246.8 49.9 all-reduce.22
where the time goes:
time: 311 us; the launch traced here: 306 us
  matrix products  85.1 us (27%)
  waiting for transfers between devices  72.8 us (23%)
  local copies, waits for them, and re-layouts  41.1 us (13%)
  starting transfers between devices  34.6 us (11%)
  other arithmetic  34.2 us (11%)
  blocking collectives  18.6 us (6%)
  between operations  18.5 us (6%)
    dot_general x12, matrix products, advance(): before = jnp.dot(lower, log_keep, precision=highest)  49.7 us
    dot_general x12, matrix products, advance(): gathered = gathered + jnp.dot(tinted, weights, precision=highest)  33.9 us
    psum x1, waiting for transfers between devices, body(): geo_grad, sh_grad = lax.psum((geo_local, sh_local), 'tile')  31 us
    all_to_all x1, starting transfers between devices, body(): lax.all_to_all(outgoing.reshape(2, sub_count, capacity), 'sub', split_axi...  19.7 us
    psum x1, blocking collectives, body(): geo_grad, sh_grad = lax.psum((geo_local, sh_local), 'tile')  18.6 us
    all_to_all x1, waiting for transfers between devices, body(): lax.all_to_all(partials.reshape(5, sub_count, capacity), 'sub', split_axi...  15.9 us
    all_to_all x1, waiting for transfers between devices, body(): lax.all_to_all(outgoing_cot.reshape(5, sub_count, capacity), 'sub', split...  15.7 us
    reduce_sum x4, other arithmetic, advance(): offset_y = coords[1][None, :] - shapes[1][:, None]  12.1 us
  transfers between devices with their start and end apart: 4, of which 4 were waited for; matrix products, arithmetic and copies ran while one was open for 1% of the time, Pallas kernels for 0%

commit v1 on v0

v1 whole, which is shorter than its diff:
```python
import jax
import jax.numpy as jnp
from jax import lax
from jax.experimental import pallas as pl
from jax.experimental.pallas import tpu as pltpu
from jax.sharding import PartitionSpec as P

NZ, NX, NC, NT = 16, 4, 2, 4
PLANE = NX * NC
BLOCK, NLIST, LISTED, RAYS = 128, 4, 8, 256
LIVE = NLIST * BLOCK
LOG2E = 1.4426950408889634
f32, i32, bf16 = jnp.float32, jnp.int32, jnp.bfloat16
highest = lax.Precision.HIGHEST
UF, UB = 4, 8


def iota(shape, axis):
    return lax.broadcasted_iota(i32, shape, axis)


def take(table, index):
    return jnp.take_along_axis(table, index, axis=1, mode="promise_in_bounds")


def group_swap(tiles):
    lane = iota((8, 128), 1)
    low = lane < 64
    even = (lane // 32) % 2 == 0
    a, b, c, d = tiles
    a, c = jnp.where(low, a, pltpu.roll(c, 64, 1)), jnp.where(low, pltpu.roll(a, 64, 1), c)
    b, d = jnp.where(low, b, pltpu.roll(d, 64, 1)), jnp.where(low, pltpu.roll(b, 64, 1), d)
    a, b = jnp.where(even, a, pltpu.roll(b, 32, 1)), jnp.where(even, pltpu.roll(a, 96, 1), b)
    c, d = jnp.where(even, c, pltpu.roll(d, 32, 1)), jnp.where(even, pltpu.roll(c, 96, 1), d)
    return a, b, c, d


def pair_merge(first, second):
    low = iota((8, 128), 1) < 64
    return (
        jnp.where(low, first, pltpu.roll(second, 64, 1)),
        jnp.where(low, pltpu.roll(first, 64, 1), second),
    )


def harmonic_rows(angles):
    shape = (8 * NT, 128)
    view = iota(shape, 0) // 8
    row = iota(shape, 1)
    azimuth = jnp.zeros(shape, f32)
    elevation = jnp.zeros(shape, f32)
    for v in range(NT):
        azimuth = jnp.where(view == v, angles[v, 0], azimuth)
        elevation = jnp.where(view == v, angles[v, 1], elevation)
    x = jnp.cos(elevation) * jnp.cos(azimuth)
    y = jnp.cos(elevation) * jnp.sin(azimuth)
    z = jnp.sin(elevation)
    xx, yy, zz = x * x, y * y, z * z
    terms = [
        0.28209479177387814 * jnp.ones_like(x),
        -0.4886025119029199 * y,
        0.4886025119029199 * z,
        -0.4886025119029199 * x,
        1.0925484305920792 * x * y,
        -1.0925484305920792 * y * z,
        0.31539156525252005 * (2.0 * zz - xx - yy),
        -1.0925484305920792 * x * z,
        0.5462742152960396 * (xx - yy),
        -0.5900435899266435 * y * (3.0 * xx - yy),
        2.890611442640554 * x * y * z,
        -0.4570457994644658 * y * (4.0 * zz - xx - yy),
        0.3731763325901154 * z * (2.0 * zz - 3.0 * xx - 3.0 * yy),
        -0.4570457994644658 * x * (4.0 * zz - xx - yy),
        1.445305721320277 * z * (xx - yy),
        -0.5900435899266435 * x * (xx - 3.0 * yy),
    ]
    out = jnp.zeros(shape, f32)
    for k, term in enumerate(terms):
        out = jnp.where(row // 3 == k, term, out)
    return jnp.where((row % 3 == iota(shape, 0) % 8) & (row < 48), out, 0.0)


def kernel(
    angles, ids, counts, cot_ref, lists_ref, geo_hbm, sh_hbm,
    pay_out, har_out,
    geo_s, sh_s, cum_s, rank_s, slot_s,
    zs_i, zr_i, zs_c, zr_c, xs_i, xr_i, xs_c, xr_c,
    xs_2, xr_2, zs_2, zr_2, zs_3, zr_3, xs_3, xr_3,
    rows_s, alpha_s, weight_s, tint_s, acc_s, red_s, cot_s, pay_s, pay_r,
    zsend, zrecv, xsend, xrecv, ysend, yrecv, lsem,
):
    me = lax.axis_index("sub")
    view = lax.axis_index("tile")
    mz = me // PLANE
    mp = me % PLANE

    def far(i):
        return (mz + 8 + ((i + 1) // 2) * (1 - 2 * (i % 2)) + NZ) % NZ

    barrier = pltpu.get_barrier_semaphore()

    def greet_z(i, c):
        pl.semaphore_signal(barrier, inc=1, device_id={"sub": far(i) * PLANE + mp})
        return c

    def greet_p(i, c):
        pl.semaphore_signal(barrier, inc=1, device_id={"sub": mz * PLANE + (mp + 1 + i) % PLANE})
        return c

    def greet_y(i, c):
        pl.semaphore_signal(barrier, inc=1, device_id={"tile": (view + 1 + i) % NT})
        return c

    lax.fori_loop(0, NZ - 1, greet_z, 0)
    lax.fori_loop(0, PLANE - 1, greet_p, 0)
    lax.fori_loop(0, NT - 1, greet_y, 0)

    geo_copy = pltpu.make_async_copy(geo_hbm, geo_s, lsem.at[0])
    sh_copy = pltpu.make_async_copy(sh_hbm, sh_s, lsem.at[1])
    geo_copy.start()
    sh_copy.start()

    def z_copy(src, dst, phase, other):
        return pltpu.make_async_remote_copy(
            src_ref=src.at[:, other, :],
            dst_ref=dst.at[:, mz, :],
            send_sem=zsend.at[phase, other],
            recv_sem=zrecv.at[phase, mz],
            device_id={"sub": other * PLANE + mp},
        )

    def z_start(src, dst, phase):
        pltpu.make_async_copy(src.at[:, mz, :], dst.at[:, mz, :], zrecv.at[phase, mz]).start()

        def go(i, c):
            z_copy(src, dst, phase, far(i)).start()
            return c

        lax.fori_loop(0, NZ - 1, go, 0)

    def z_wait(src, dst, phase):
        pltpu.make_async_copy(src.at[:, mz, :], dst.at[:, mz, :], zrecv.at[phase, mz]).wait()

        def go(i, c):
            other = (mz + 1 + i) % NZ
            pltpu.make_async_remote_copy(
                src_ref=src.at[:, other, :],
                dst_ref=dst.at[:, other, :],
                send_sem=zsend.at[phase, other],
                recv_sem=zrecv.at[phase, other],
                device_id={"sub": other * PLANE + mp},
            ).wait_recv()
            return c

        lax.fori_loop(0, NZ - 1, go, 0)

    def z_drain(src, dst, phase):
        def go(i, c):
            z_copy(src, dst, phase, (mz + 1 + i) % NZ).wait_send()
            return c

        lax.fori_loop(0, NZ - 1, go, 0)

    def x_copy(src, dst, phase, other):
        return pltpu.make_async_remote_copy(
            src_ref=src.at[other],
            dst_ref=dst.at[mp],
            send_sem=xsend.at[phase, other],
            recv_sem=xrecv.at[phase, mp],
            device_id={"sub": mz * PLANE + other},
        )

    def x_start(src, dst, phase):
        pltpu.make_async_copy(src.at[mp], dst.at[mp], xrecv.at[phase, mp]).start()

        def go(i, c):
            x_copy(src, dst, phase, (mp + 1 + i) % PLANE).start()
            return c

        lax.fori_loop(0, PLANE - 1, go, 0)

    def x_wait(src, dst, phase):
        pltpu.make_async_copy(src.at[mp], dst.at[mp], xrecv.at[phase, mp]).wait()

        def go(i, c):
            other = (mp + 1 + i) % PLANE
            pltpu.make_async_remote_copy(
                src_ref=src.at[other],
                dst_ref=dst.at[other],
                send_sem=xsend.at[phase, other],
                recv_sem=xrecv.at[phase, other],
                device_id={"sub": mz * PLANE + other},
            ).wait_recv()
            return c

        lax.fori_loop(0, PLANE - 1, go, 0)

    def x_drain(src, dst, phase):
        def go(i, c):
            x_copy(src, dst, phase, (mp + 1 + i) % PLANE).wait_send()
            return c

        lax.fori_loop(0, PLANE - 1, go, 0)

    lists = lists_ref[...]
    row = iota((128, RAYS), 0)
    named = (row % 16) * 8 + ((row // 16) % 2) * 4 + row // 32
    hit = jnp.zeros((128, RAYS), f32)
    for k in range(LISTED):
        hit = jnp.where(lists[k : k + 1, :] == named, 1.0, hit)
    upper = jnp.where(iota((RAYS, RAYS), 0) <= iota((RAYS, RAYS), 1), 1.0, 0.0).astype(bf16)
    cum = jnp.dot(hit.astype(bf16), upper, preferred_element_type=f32)
    cum_s[...] = cum
    rank_s[...] = jnp.minimum((cum - hit).astype(i32), 31)

    lane = iota((32, 128), 1)
    group = lane // 32
    want = (lane % 32).astype(f32)
    spot = jnp.zeros((32, 128), i32)
    half = jnp.zeros((32, 128), i32)
    valid = jnp.zeros((32, 128), i32)
    for q in range(4):
        left = cum_s[32 * q : 32 * q + 32, 0:128]
        right = cum_s[32 * q : 32 * q + 32, 128:256]
        in_right = left[:, 127:128] <= want
        pos = jnp.zeros((32, 128), i32)
        for step in (64, 32, 16, 8, 4, 2, 1):
            probe = pos + (step - 1)
            seen = jnp.where(in_right, take(right, probe), take(left, probe))
            pos = jnp.where(seen <= want, pos + step, pos)
        here = group == q
        spot = jnp.where(here, pos, spot)
        half = jnp.where(here & in_right, 1, half)
        valid = jnp.where(here & (want < right[:, 127:128]), 1, valid)
    slot_s[0] = spot
    slot_s[1] = half
    slot_s[2] = valid
    index = (spot + 128 * half).astype(f32)
    for h in range(2):
        zs_i[h] = index[16 * h : 16 * h + 16, :]
    for j in range(4):
        left = jnp.broadcast_to(cot_ref[j : j + 1, 0:128], (32, 128))
        right = jnp.broadcast_to(cot_ref[j : j + 1, 128:256], (32, 128))
        picked = jnp.where(half == 1, take(right, spot), take(left, spot))
        for h in range(2):
            zs_c[2 * j + h] = picked[16 * h : 16 * h + 16, :]

    pl.semaphore_wait(barrier, NZ - 1 + PLANE - 1 + NT - 1)
    z_start(zs_i, zr_i, 0)
    z_start(zs_c, zr_c, 1)

    harmonics = harmonic_rows(angles)
    har_out[...] = harmonics
    cot_s[0:32, :] = harmonics
    geo_copy.wait()
    sh_copy.wait()
    own = cot_s[pl.ds(pl.multiple_of(view * 8, 8), 8), :]
    for l in range(NLIST):
        chosen = jnp.full((1, BLOCK), ids[l], i32)
        block = geo_s[:, 0:BLOCK]
        coef = sh_s[:, 0:BLOCK]
        for b in range(1, geo_s.shape[1] // BLOCK):
            match = chosen == b
            block = jnp.where(match, geo_s[:, b * BLOCK : (b + 1) * BLOCK], block)
            coef = jnp.where(match, sh_s[:, b * BLOCK : (b + 1) * BLOCK], coef)
        colour = 0.5 + jnp.dot(own[:, 0:48], coef, precision=highest)
        live = jnp.full((1, BLOCK), counts[0], i32) > l
        fade = jnp.where(live, jnp.log(block[5:6]) * LOG2E, -1e30)
        rows = jnp.concatenate(
            [
                block[0:2],
                block[2:3] * (-0.5 * LOG2E),
                block[3:4] * (-LOG2E),
                block[4:5] * (-0.5 * LOG2E),
                fade,
                colour[0:3],
                block[6:7],
                jnp.zeros((6, BLOCK), f32),
            ],
            axis=0,
        )
        pay_s[0:7, l * BLOCK : (l + 1) * BLOCK] = block
        turned = jnp.transpose(rows)
        for p in range(10):
            rows_s[p, l * BLOCK : (l + 1) * BLOCK, :] = jnp.broadcast_to(
                turned[:, p : p + 1], (BLOCK, 128)
            )

    z_wait(zs_i, zr_i, 0)
    for h in range(2):
        top, bottom = zr_i[h, 0:8, :], zr_i[h, 8:16, :]
        for q, tile in enumerate(group_swap((top, bottom, top, bottom))):
            xs_i[h * 4 + q] = tile
    x_start(xs_i, xr_i, 0)
    z_wait(zs_c, zr_c, 1)
    for j in (0, 2):
        for h in range(2):
            tiles = [zr_c[2 * a + h, 8 * b : 8 * b + 8, :] for a in (j, j + 1) for b in (0, 1)]
            for q, tile in enumerate(group_swap(tiles)):
                xs_c[h * 4 + q, 4 * j : 4 * j + 8, :] = tile
    x_start(xs_c, xr_c, 1)
    x_wait(xs_i, xr_i, 0)

    sub8 = iota((8, 128), 0)
    lane8 = iota((8, 128), 1)
    ys = (2 * (8 * ((lane8 // 32) % 2) + sub8) + lane8 // 64).astype(f32)
    xs = []
    for v in range(4):
        first, _ = pair_merge(xr_i[v], xr_i[4 + v])
        xs.append(first + 256.0 * v)
    x_wait(xs_c, xr_c, 1)
    for j in (0, 2):
        for v in range(4):
            first, second = pair_merge(
                xr_c[v, 4 * j : 4 * j + 8, :], xr_c[4 + v, 4 * j : 4 * j + 8, :]
            )
            cot_s[(j * 4 + v) * 8 : (j * 4 + v) * 8 + 8, :] = first
            cot_s[((j + 1) * 4 + v) * 8 : ((j + 1) * 4 + v) * 8 + 8, :] = second

    def bits(p, g):
        return rows_s[p, pl.ds(g, 8, stride=0), :]

    cots = [[cot_s[(j * 4 + v) * 8 : (j * 4 + v) * 8 + 8, :] for v in range(4)] for j in range(4)]

    def ahead(step, carry):
        passing = list(carry[0:4])
        gathered = list(carry[4:8])
        for u in range(UF):
            g = step * UF + u
            mx, my, ca, cb, cc, fade = [bits(p, g) for p in range(6)]
            tint = [bits(6 + j, g) for j in range(4)]
            dy = ys - my
            cross = cb * dy
            base = cc * dy * dy + fade
            for v in range(4):
                dx = xs[v] - mx
                alpha = jnp.exp2((ca * dx + cross) * dx + base)
                weight = alpha * passing[v]
                passing[v] = passing[v] - weight
                shade = tint[0] * cots[0][v]
                for j in range(1, 4):
                    shade = shade + tint[j] * cots[j][v]
                gathered[v] = gathered[v] + weight * shade
                alpha_s[g, v] = alpha
                weight_s[g, v] = weight
                tint_s[g, v] = shade
        return tuple(passing) + tuple(gathered)

    start = tuple(jnp.ones((8, 128), f32) for _ in range(4)) + tuple(
        jnp.zeros((8, 128), f32) for _ in range(4)
    )
    done = lax.fori_loop(0, LIVE // UF, ahead, start)
    passing, gathered = done[0:4], done[4:8]

    for v in range(4):
        xs_2[v], xs_2[4 + v] = pair_merge(gathered[v], passing[v])
    x_start(xs_2, xr_2, 2)
    x_wait(xs_2, xr_2, 2)
    for h in range(2):
        tiles = group_swap([xr_2[h * 4 + q] for q in range(4)])
        for a in range(2):
            for b in range(2):
                zs_2[2 * a + h, 8 * b : 8 * b + 8, :] = tiles[2 * a + b]
    z_start(zs_2, zr_2, 2)
    z_wait(zs_2, zr_2, 2)

    lists = lists_ref[...]
    table = [jnp.concatenate([zr_2[2 * a], zr_2[2 * a + 1]], axis=0) for a in range(2)]
    rowq = iota((32, RAYS), 0)
    picked = [[jnp.zeros((32, RAYS), f32) for _ in range(LISTED)] for _ in range(2)]
    for q in range(4):
        named_q = (rowq % 16) * 8 + (rowq // 16) * 4 + q
        place = rank_s[32 * q : 32 * q + 32, :] + 32 * q
        found = [
            jnp.concatenate([take(table[a], place[:, 0:128]), take(table[a], place[:, 128:256])], axis=1)
            for a in range(2)
        ]
        for k in range(LISTED):
            match = lists[k : k + 1, :] == named_q
            for a in range(2):
                picked[a][k] = jnp.where(match, found[a], picked[a][k])
    entry = [[jnp.sum(picked[a][k], axis=0, keepdims=True) for k in range(LISTED)] for a in range(2)]
    carried = [jnp.ones((1, RAYS), f32)]
    for k in range(LISTED):
        carried.append(carried[k] * entry[1][k])
    behind = [None] * LISTED
    tail = jnp.zeros((1, RAYS), f32)
    for k in reversed(range(LISTED)):
        behind[k] = carried[k] * tail
        tail = entry[0][k] + entry[1][k] * tail

    spot, half, valid = slot_s[0], slot_s[1], slot_s[2]
    sent = [jnp.zeros((32, 128), f32) for _ in range(2)]
    for q in range(4):
        named_q = (rowq % 16) * 8 + (rowq // 16) * 4 + q
        dense = [jnp.zeros((32, RAYS), f32) for _ in range(2)]
        for k in range(LISTED):
            match = lists[k : k + 1, :] == named_q
            dense[0] = jnp.where(match, carried[k], dense[0])
            dense[1] = jnp.where(match, behind[k], dense[1])
        keep = (group == q) & (valid == 1)
        for a in range(2):
            got = jnp.where(half == 1, take(dense[a][:, 128:256], spot), take(dense[a][:, 0:128], spot))
            sent[a] = jnp.where(keep, got, sent[a])
    for a in range(2):
        for h in range(2):
            zs_3[2 * a + h] = sent[a][16 * h : 16 * h + 16, :]
    z_start(zs_3, zr_3, 3)
    z_wait(zs_3, zr_3, 3)
    for h in range(2):
        tiles = [zr_3[2 * a + h, 8 * b : 8 * b + 8, :] for a in range(2) for b in range(2)]
        for q, tile in enumerate(group_swap(tiles)):
            xs_3[h * 4 + q] = tile
    x_start(xs_3, xr_3, 3)
    x_wait(xs_3, xr_3, 3)
    scale, rest = [], []
    for v in range(4):
        first, second = pair_merge(xr_3[v], xr_3[4 + v])
        scale.append(first)
        rest.append(second)
    for j in range(4):
        for v in range(4):
            at = (j * 4 + v) * 8
            cot_s[at : at + 8, :] = cot_s[at : at + 8, :] * scale[v]
    lit = [[cot_s[(j * 4 + v) * 8 : (j * 4 + v) * 8 + 8, :] for v in range(4)] for j in range(4)]

    def back(step, carry):
        behind = list(carry)
        first = (LIVE // UB - 1 - step) * UB
        for u in reversed(range(UB)):
            g = first + u
            mx, my = bits(0, g), bits(1, g)
            dy = ys - my
            total = total_x = total_xx = None
            tints = [None] * 4
            for v in range(4):
                alpha = alpha_s[g, v]
                weight = weight_s[g, v]
                gap = scale[v] * tint_s[g, v] - behind[v]
                behind[v] = behind[v] + alpha * gap
                d = weight * gap
                dx = xs[v] - mx
                d_x = d * dx
                d_xx = d_x * dx
                lights = [weight * lit[j][v] for j in range(4)]
                if v == 0:
                    total, total_x, total_xx, tints = d, d_x, d_xx, lights
                else:
                    total, total_x, total_xx = total + d, total_x + d_x, total_xx + d_xx
                    tints = [s + t for s, t in zip(tints, lights)]
            total_y = total * dy
            sums = [total, total_x, total_xx, total_y, total_y * dy, total_x * dy] + tints
            for p, s in enumerate(sums):
                acc_s[p, 8 * u : 8 * u + 8, :] = s
        for p in range(10):
            folded = acc_s[p, pl.ds(0, 8, stride=8), :]
            for i in range(1, 8):
                folded = folded + acc_s[p, pl.ds(i, 8, stride=8), :]
            red_s[p, pl.ds(pl.multiple_of(first, 8), 8), :] = folded
        return tuple(behind)

    lax.fori_loop(0, LIVE // UB, back, tuple(rest))

    row16 = iota((16, 128), 0)
    moments = jnp.zeros((16, LIVE), f32)
    for p in range(10):
        ones = jnp.where(row16 == p, 1.0, 0.0).astype(bf16)
        whole = red_s[p]
        high = whole.astype(bf16)
        low = (whole - high.astype(f32)).astype(bf16)
        for part in (high, low):
            moments = moments + lax.dot_general(
                ones, part, (((1,), (1,)), ((), ())), preferred_element_type=f32
            )
    s0, sx, sxx, sy, syy, sxy = [moments[p : p + 1] for p in range(6)]
    ga, gb, gc, go = [pay_s[p : p + 1, :] for p in (2, 3, 4, 5)]
    block_row = jnp.concatenate(
        [jnp.full((1, BLOCK), ids[l].astype(f32), f32) for l in range(NLIST)], axis=1
    )
    payload = jnp.concatenate(
        [
            ga * sx + gb * sy,
            gb * sx + gc * sy,
            -0.5 * sxx,
            -sxy,
            -0.5 * syy,
            s0 / go,
            moments[9:10],
            block_row,
            moments[6:9],
            jnp.zeros((5, LIVE), f32),
        ],
        axis=0,
    )
    pay_s[...] = payload

    def y_copy(other):
        return pltpu.make_async_remote_copy(
            src_ref=pay_s,
            dst_ref=pay_r.at[view],
            send_sem=ysend.at[other],
            recv_sem=yrecv.at[view],
            device_id={"tile": other},
        )

    own_copy = pltpu.make_async_copy(pay_s, pay_r.at[view], yrecv.at[view])
    own_copy.start()
    for i in range(NT - 1):
        y_copy((view + 1 + i) % NT).start()
    z_drain(zs_i, zr_i, 0)
    z_drain(zs_c, zr_c, 1)
    z_drain(zs_2, zr_2, 2)
    z_drain(zs_3, zr_3, 3)
    x_drain(xs_i, xr_i, 0)
    x_drain(xs_c, xr_c, 1)
    x_drain(xs_2, xr_2, 2)
    x_drain(xs_3, xr_3, 3)
    own_copy.wait()
    for i in range(NT - 1):
        other = (view + 1 + i) % NT
        pltpu.make_async_remote_copy(
            src_ref=pay_s,
            dst_ref=pay_r.at[other],
            send_sem=ysend.at[other],
            recv_sem=yrecv.at[other],
            device_id={"tile": other},
        ).wait()
    pay_out[...] = pay_r[...]


def expand(pay, har, geo_out, sh_out, tint_s):
    tops = [[pay[v, 0:8, l * BLOCK : (l + 1) * BLOCK] for l in range(NLIST)] for v in range(NT)]
    for b in range(geo_out.shape[1] // BLOCK):
        cols = slice(b * BLOCK, (b + 1) * BLOCK)
        geo = jnp.zeros((8, BLOCK), f32)
        for v in range(NT):
            tint = jnp.zeros((8, BLOCK), f32)
            for l in range(NLIST):
                match = tops[v][l][7:8, :] == float(b)
                geo = geo + jnp.where(match, tops[v][l], 0.0)
                tint = tint + jnp.where(match, pay[v, 8:16, l * BLOCK : (l + 1) * BLOCK], 0.0)
            tint_s[8 * v : 8 * v + 8, cols] = tint
        geo_out[:, cols] = geo[0:7]
    sh_out[...] = lax.dot_general(
        har[:, 0:48], tint_s[...], (((0,), (0,)), ((), ())),
        precision=highest, preferred_element_type=f32,
    )


def body(ray_cot, ray_lists, geometry, sh_coef, view_angles, block_ids, block_counts):
    resident = geometry.shape[1]
    vmem = pl.BlockSpec(memory_space=pltpu.VMEM)
    smem = pl.BlockSpec(memory_space=pltpu.SMEM)
    hbm = pl.BlockSpec(memory_space=pl.ANY)

    def room(*shape):
        return pltpu.VMEM(shape, f32)

    z_pair = lambda n: [room(n, NZ, 128), room(n, NZ, 128)]
    x_pair = lambda n: [room(PLANE, n, 128), room(PLANE, n, 128)]
    payload, harmonics = pl.pallas_call(
        kernel,
        out_shape=(
            jax.ShapeDtypeStruct((NT, 16, LIVE), f32),
            jax.ShapeDtypeStruct((8 * NT, 128), f32),
        ),
        in_specs=[smem, smem, smem, vmem, vmem, hbm, hbm],
        out_specs=(vmem, vmem),
        scratch_shapes=[
            room(7, resident), room(48, resident), room(128, RAYS),
            pltpu.VMEM((128, RAYS), i32), pltpu.VMEM((3, 32, 128), i32),
            *z_pair(2), *z_pair(8), *x_pair(8), *x_pair(16),
            *x_pair(8), *z_pair(4), *z_pair(4), *x_pair(8),
            room(10, LIVE, 128), room(LIVE, 4, 8, 128), room(LIVE, 4, 8, 128),
            room(LIVE, 4, 8, 128), room(10, 64, 128), room(10, LIVE, 128),
            room(128, 128), room(16, LIVE), room(NT, 16, LIVE),
            pltpu.SemaphoreType.DMA((4, NZ)), pltpu.SemaphoreType.DMA((4, NZ)),
            pltpu.SemaphoreType.DMA((4, PLANE)), pltpu.SemaphoreType.DMA((4, PLANE)),
            pltpu.SemaphoreType.DMA((NT,)), pltpu.SemaphoreType.DMA((NT,)),
            pltpu.SemaphoreType.DMA((2,)),
        ],
        compiler_params=pltpu.CompilerParams(collective_id=0, has_side_effects=True),
        name="splat",
    )(
        view_angles, block_ids[0, 0], block_counts[0], ray_cot[:, 0, :],
        jnp.transpose(ray_lists[0]), geometry, sh_coef,
    )
    return pl.pallas_call(
        expand,
        out_shape=(
            jax.ShapeDtypeStruct((7, resident), f32),
            jax.ShapeDtypeStruct((48, resident), f32),
        ),
        in_specs=[vmem, vmem],
        out_specs=(vmem, vmem),
        scratch_shapes=[room(8 * NT, resident)],
        name="expand",
    )(payload, harmonics)


def solution(mesh):
    return jax.shard_map(
        body,
        mesh=mesh,
        in_specs=(
            P(None, "tile", "sub"),
            P("tile", "sub", None),
            P(None, "sub"),
            P(None, "sub"),
            P(),
            P("sub", "tile", None),
            P("sub", "tile"),
        ),
        out_specs=(P(None, "sub"), P(None, "sub")),
        check_vma=False,
    )
```

time: 311 us -> 79.5 us (0.26)
  the two profiles are of different devices: /device:TPU:4 before, /device:TPU:1 now
where the time goes in v1:
time: 79.5 us; the launch traced here: 79.3 us
  Pallas kernels  76 us (96%)
  local copies, waits for them, and re-layouts  1.94 us (2%)
  between operations  1.3 us (2%)
    pallas_call x1, Pallas kernels, body(): pl.pallas_call(kernel, out_shape=(jax.ShapeDtypeStruct((NT, 16, LIVE), f3...  73.8 us
    pallas_call x1, Pallas kernels, body(): pl.pallas_call(expand, out_shape=(jax.ShapeDtypeStruct((7, resident), f32...  2.19 us
    unnamed x6, local copies, waits for them, and re-layouts  1.94 us

profile of v1, /device:TPU:1, one launch (start us, length us, event | category | flops | bytes accessed | tf_op | source)
XLA Modules:
  0.0 79.3 jit_solution(8872456461994703453)
XLA Ops:
  1.3 0.0 copy-start
  1.3 0.0 copy-start.1
  1.3 0.7 copy-done.1
  2.0 0.7 copy.9.angles
  2.6 0.0 copy-done
  2.6 0.6 copy.12
  3.2 73.8 %splat.1 = (f32[4,16,512]{2,1,0:T(8,128)}, f32[32,128]{1,0:T(8,128)}) custom-call(f32[4,2]{1,0:T(4,128)} %copy.9.angles, s32[4]{0:T(128)} %bitcast.11, s32[1]{0:T(128)} %bitcast.8.counts, f32[4,256]{1,0:T(4,128)} %bitcast.9, s32[8,256]{1,0:T(8,128)} %bitcast.10, f32[7,2048]{1,0:T(8,128)} %geo_hbm.1, f32[48,2048]{1,0:T(8,128)} %sh_hbm.1), custom_call_target="tpu_custom_call" | custom-call | tf_op jit(solution)/shard_map/splat/pallas_call | solution.py:561
  77.1 2.2 %expand.1 = (f32[7,2048]{1,0:T(8,128)}, f32[48,2048]{1,0:T(8,128)}) custom-call(f32[4,16,512]{2,1,0:T(8,128)} %get-tuple-element.4.pay, f32[32,128]{1,0:T(8,128)} %get-tuple-element.5.har), custom_call_target="tpu_custom_call" | custom-call | tf_op jit(solution)/shard_map/expand/pallas_call | solution.py:588
Async XLA Ops:
  1.3 1.4 %copy-start = (f32[4,1,256]{2,1,0:T(1,128)S(1)}, f32[4,1,256]{2,1,0:T(1,128)}, u32[]{:S(2)}) copy-start(f32[4,1,256]{2,1,0:T(1,128)} %param.7) | copy-start | bytes 12292
  1.3 0.7 copy-start.1

commit v2 on v1

--- a/solution.py
+++ b/solution.py
@@ -12,7 +12,7 @@
 LOG2E = 1.4426950408889634
 f32, i32, bf16 = jnp.float32, jnp.int32, jnp.bfloat16
 highest = lax.Precision.HIGHEST
-UF, UB = 4, 8
+UF, UB = 8, 16
 
 
 def iota(shape, axis):
@@ -50,8 +50,8 @@
     azimuth = jnp.zeros(shape, f32)
     elevation = jnp.zeros(shape, f32)
     for v in range(NT):
-        azimuth = jnp.where(view == v, angles[v, 0], azimuth)
-        elevation = jnp.where(view == v, angles[v, 1], elevation)
+        azimuth = jnp.where(view == v, jnp.broadcast_to(angles[0:1, v : v + 1], shape), azimuth)
+        elevation = jnp.where(view == v, jnp.broadcast_to(angles[1:2, v : v + 1], shape), elevation)
     x = jnp.cos(elevation) * jnp.cos(azimuth)
     y = jnp.cos(elevation) * jnp.sin(azimuth)
     z = jnp.sin(elevation)
@@ -81,12 +81,13 @@
 
 
 def kernel(
-    angles, ids, counts, cot_ref, lists_ref, geo_hbm, sh_hbm,
+    angles_hbm, ids_hbm, counts, ray_cot_hbm, lists_hbm, geo_hbm, sh_hbm,
     pay_out, har_out,
+    angles_s, ids_s, ray_cot_s, lists_ref,
     geo_s, sh_s, cum_s, rank_s, slot_s,
     zs_i, zr_i, zs_c, zr_c, xs_i, xr_i, xs_c, xr_c,
     xs_2, xr_2, zs_2, zr_2, zs_3, zr_3, xs_3, xr_3,
-    rows_s, alpha_s, weight_s, tint_s, acc_s, red_s, cot_s, pay_s, pay_r,
+    rows_s, alpha_s, weight_s, tint_s, high_s, low_s, red_s, cot_s, pay_s, pay_r,
     zsend, zrecv, xsend, xrecv, ysend, yrecv, lsem,
 ):
     me = lax.axis_index("sub")
@@ -115,10 +116,19 @@
     lax.fori_loop(0, PLANE - 1, greet_p, 0)
     lax.fori_loop(0, NT - 1, greet_y, 0)
 
-    geo_copy = pltpu.make_async_copy(geo_hbm, geo_s, lsem.at[0])
-    sh_copy = pltpu.make_async_copy(sh_hbm, sh_s, lsem.at[1])
-    geo_copy.start()
-    sh_copy.start()
+    fetches = [
+        pltpu.make_async_copy(src, dst, lsem.at[n])
+        for n, (src, dst) in enumerate(
+            [
+                (lists_hbm, lists_ref), (ray_cot_hbm, ray_cot_s), (angles_hbm, angles_s),
+                (ids_hbm, ids_s), (geo_hbm, geo_s), (sh_hbm, sh_s),
+            ]
+        )
+    ]
+    for fetch in fetches:
+        fetch.start()
+    for fetch in fetches[0:2]:
+        fetch.wait()
 
     def z_copy(src, dst, phase, other):
         return pltpu.make_async_remote_copy(
@@ -239,24 +249,20 @@
     for h in range(2):
         zs_i[h] = index[16 * h : 16 * h + 16, :]
     for j in range(4):
-        left = jnp.broadcast_to(cot_ref[j : j + 1, 0:128], (32, 128))
-        right = jnp.broadcast_to(cot_ref[j : j + 1, 128:256], (32, 128))
+        left = jnp.broadcast_to(ray_cot_s[j][:, 0:128], (32, 128))
+        right = jnp.broadcast_to(ray_cot_s[j][:, 128:256], (32, 128))
         picked = jnp.where(half == 1, take(right, spot), take(left, spot))
         for h in range(2):
             zs_c[2 * j + h] = picked[16 * h : 16 * h + 16, :]
 
-    pl.semaphore_wait(barrier, NZ - 1 + PLANE - 1 + NT - 1)
-    z_start(zs_i, zr_i, 0)
-    z_start(zs_c, zr_c, 1)
-
-    harmonics = harmonic_rows(angles)
+    for fetch in fetches[2:]:
+        fetch.wait()
+    harmonics = harmonic_rows(angles_s)
     har_out[...] = harmonics
     cot_s[0:32, :] = harmonics
-    geo_copy.wait()
-    sh_copy.wait()
     own = cot_s[pl.ds(pl.multiple_of(view * 8, 8), 8), :]
     for l in range(NLIST):
-        chosen = jnp.full((1, BLOCK), ids[l], i32)
+        chosen = jnp.broadcast_to(ids_s[0][:, l : l + 1], (1, BLOCK))
         block = geo_s[:, 0:BLOCK]
         coef = sh_s[:, 0:BLOCK]
         for b in range(1, geo_s.shape[1] // BLOCK):
@@ -264,7 +270,7 @@
             block = jnp.where(match, geo_s[:, b * BLOCK : (b + 1) * BLOCK], block)
             coef = jnp.where(match, sh_s[:, b * BLOCK : (b + 1) * BLOCK], coef)
         colour = 0.5 + jnp.dot(own[:, 0:48], coef, precision=highest)
-        live = jnp.full((1, BLOCK), counts[0], i32) > l
+        live = jnp.full((1, BLOCK), counts[0, 0], i32) > l
         fade = jnp.where(live, jnp.log(block[5:6]) * LOG2E, -1e30)
         rows = jnp.concatenate(
             [
@@ -279,12 +285,17 @@
             ],
             axis=0,
         )
-        pay_s[0:7, l * BLOCK : (l + 1) * BLOCK] = block
+        pay_s[l, 0:7, :] = block
+        pay_s[l, 7:8, :] = chosen.astype(f32)
         turned = jnp.transpose(rows)
         for p in range(10):
             rows_s[p, l * BLOCK : (l + 1) * BLOCK, :] = jnp.broadcast_to(
                 turned[:, p : p + 1], (BLOCK, 128)
             )
+
+    pl.semaphore_wait(barrier, NZ - 1 + PLANE - 1 + NT - 1)
+    z_start(zs_i, zr_i, 0)
+    z_start(zs_c, zr_c, 1)
 
     z_wait(zs_i, zr_i, 0)
     for h in range(2):
@@ -424,89 +435,91 @@
             cot_s[at : at + 8, :] = cot_s[at : at + 8, :] * scale[v]
     lit = [[cot_s[(j * 4 + v) * 8 : (j * 4 + v) * 8 + 8, :] for v in range(4)] for j in range(4)]
 
-    def back(step, carry):
-        behind = list(carry)
-        first = (LIVE // UB - 1 - step) * UB
-        for u in reversed(range(UB)):
-            g = first + u
-            mx, my = bits(0, g), bits(1, g)
-            dy = ys - my
-            total = total_x = total_xx = None
-            tints = [None] * 4
-            for v in range(4):
-                alpha = alpha_s[g, v]
-                weight = weight_s[g, v]
-                gap = scale[v] * tint_s[g, v] - behind[v]
-                behind[v] = behind[v] + alpha * gap
-                d = weight * gap
-                dx = xs[v] - mx
-                d_x = d * dx
-                d_xx = d_x * dx
-                lights = [weight * lit[j][v] for j in range(4)]
-                if v == 0:
-                    total, total_x, total_xx, tints = d, d_x, d_xx, lights
-                else:
-                    total, total_x, total_xx = total + d, total_x + d_x, total_xx + d_xx
-                    tints = [s + t for s, t in zip(tints, lights)]
-            total_y = total * dy
-            sums = [total, total_x, total_xx, total_y, total_y * dy, total_x * dy] + tints
-            for p, s in enumerate(sums):
-                acc_s[p, 8 * u : 8 * u + 8, :] = s
+    def fold(ref, first):
+        line = jnp.zeros((8, 128), f32)
         for p in range(10):
-            folded = acc_s[p, pl.ds(0, 8, stride=8), :]
-            for i in range(1, 8):
-                folded = folded + acc_s[p, pl.ds(i, 8, stride=8), :]
-            red_s[p, pl.ds(pl.multiple_of(first, 8), 8), :] = folded
-        return tuple(behind)
-
-    lax.fori_loop(0, LIVE // UB, back, tuple(rest))
-
-    row16 = iota((16, 128), 0)
-    moments = jnp.zeros((16, LIVE), f32)
-    for p in range(10):
-        ones = jnp.where(row16 == p, 1.0, 0.0).astype(bf16)
-        whole = red_s[p]
-        high = whole.astype(bf16)
-        low = (whole - high.astype(f32)).astype(bf16)
-        for part in (high, low):
-            moments = moments + lax.dot_general(
-                ones, part, (((1,), (1,)), ((), ())), preferred_element_type=f32
-            )
-    s0, sx, sxx, sy, syy, sxy = [moments[p : p + 1] for p in range(6)]
-    ga, gb, gc, go = [pay_s[p : p + 1, :] for p in (2, 3, 4, 5)]
-    block_row = jnp.concatenate(
-        [jnp.full((1, BLOCK), ids[l].astype(f32), f32) for l in range(NLIST)], axis=1
-    )
-    payload = jnp.concatenate(
-        [
-            ga * sx + gb * sy,
-            gb * sx + gc * sy,
-            -0.5 * sxx,
-            -sxy,
-            -0.5 * syy,
-            s0 / go,
-            moments[9:10],
-            block_row,
-            moments[6:9],
-            jnp.zeros((5, LIVE), f32),
-        ],
-        axis=0,
-    )
-    pay_s[...] = payload
-
-    def y_copy(other):
+            parts = [ref[p, 8 * i : 8 * i + 8, :] for i in range(8)]
+            while len(parts) > 1:
+                parts = [x + y for x, y in zip(parts[::2], parts[1::2])]
+            folded = parts[0]
+            line = jnp.where(lane8 == p, jnp.sum(folded, axis=1, keepdims=True), line)
+        red_s[pl.ds(pl.multiple_of(first, 8), 8), :] = line
+
+    def y_copy(other, l):
         return pltpu.make_async_remote_copy(
-            src_ref=pay_s,
-            dst_ref=pay_r.at[view],
-            send_sem=ysend.at[other],
-            recv_sem=yrecv.at[view],
+            src_ref=pay_s.at[l],
+            dst_ref=pay_r.at[view, l],
+            send_sem=ysend.at[other, l],
+            recv_sem=yrecv.at[view, l],
             device_id={"tile": other},
         )
 
-    own_copy = pltpu.make_async_copy(pay_s, pay_r.at[view], yrecv.at[view])
-    own_copy.start()
-    for i in range(NT - 1):
-        y_copy((view + 1 + i) % NT).start()
+    def y_own(l):
+        return pltpu.make_async_copy(pay_s.at[l], pay_r.at[view, l], yrecv.at[view, l])
+
+    groups = BLOCK // UB
+    state = tuple(rest)
+    for l in reversed(range(NLIST)):
+
+        def back(step, carry):
+            behind = list(carry)
+            first = l * BLOCK + (groups - 1 - step) * UB
+            fold(low_s, jnp.minimum(first + UB, LIVE - 8))
+            for u in reversed(range(UB)):
+                g = first + u
+                acc = high_s if u >= 8 else low_s
+                mx, my = bits(0, g), bits(1, g)
+                dy = ys - my
+                total = total_x = total_xx = None
+                tints = [None] * 4
+                for v in range(4):
+                    weight = weight_s[g, v]
+                    gap = scale[v] * tint_s[g, v] - behind[v]
+                    behind[v] = behind[v] + alpha_s[g, v] * gap
+                    d = weight * gap
+                    dx = xs[v] - mx
+                    d_x = d * dx
+                    d_xx = d_x * dx
+                    lights = [weight * lit[j][v] for j in range(4)]
+                    if v == 0:
+                        total, total_x, total_xx, tints = d, d_x, d_xx, lights
+                    else:
+                        total, total_x, total_xx = total + d, total_x + d_x, total_xx + d_xx
+                        tints = [s + t for s, t in zip(tints, lights)]
+                total_y = total * dy
+                sums = [total, total_x, total_xx, total_y, total_y * dy, total_x * dy] + tints
+                for p, s in enumerate(sums):
+                    acc[p, pl.ds(u % 8, 8, stride=8), :] = s
+                if u == 8:
+                    fold(high_s, first + 8)
+            return tuple(behind)
+
+        if l == NLIST - 1:
+            low_s[...] = jnp.zeros_like(low_s)
+        state = lax.fori_loop(0, groups, back, state)
+        fold(low_s, l * BLOCK)
+        moments = jnp.transpose(red_s[l * BLOCK : (l + 1) * BLOCK, :])
+        s0, sx, sxx, sy, syy, sxy = [moments[p : p + 1] for p in range(6)]
+        ga, gb, gc, go, chosen = [pay_s[l, p : p + 1, :] for p in (2, 3, 4, 5, 7)]
+        pay_s[l] = jnp.concatenate(
+            [
+                ga * sx + gb * sy,
+                gb * sx + gc * sy,
+                -0.5 * sxx,
+                -sxy,
+                -0.5 * syy,
+                s0 / go,
+                moments[9:10],
+                chosen,
+                moments[6:9],
+                jnp.zeros((5, BLOCK), f32),
+            ],
+            axis=0,
+        )
+        y_own(l).start()
+        for i in range(NT - 1):
+            y_copy((view + 1 + i) % NT, l).start()
+
     z_drain(zs_i, zr_i, 0)
     z_drain(zs_c, zr_c, 1)
     z_drain(zs_2, zr_2, 2)
@@ -515,21 +528,22 @@
     x_drain(xs_c, xr_c, 1)
     x_drain(xs_2, xr_2, 2)
     x_drain(xs_3, xr_3, 3)
-    own_copy.wait()
-    for i in range(NT - 1):
-        other = (view + 1 + i) % NT
-        pltpu.make_async_remote_copy(
-            src_ref=pay_s,
-            dst_ref=pay_r.at[other],
-            send_sem=ysend.at[other],
-            recv_sem=yrecv.at[other],
-            device_id={"tile": other},
-        ).wait()
+    for l in reversed(range(NLIST)):
+        y_own(l).wait()
+        for i in range(NT - 1):
+            other = (view + 1 + i) % NT
+            pltpu.make_async_remote_copy(
+                src_ref=pay_s.at[l],
+                dst_ref=pay_r.at[other, l],
+                send_sem=ysend.at[other, l],
+                recv_sem=yrecv.at[other, l],
+                device_id={"tile": other},
+            ).wait()
     pay_out[...] = pay_r[...]
 
 
 def expand(pay, har, geo_out, sh_out, tint_s):
-    tops = [[pay[v, 0:8, l * BLOCK : (l + 1) * BLOCK] for l in range(NLIST)] for v in range(NT)]
+    tops = [[pay[v, l, 0:8, :] for l in range(NLIST)] for v in range(NT)]
     for b in range(geo_out.shape[1] // BLOCK):
         cols = slice(b * BLOCK, (b + 1) * BLOCK)
         geo = jnp.zeros((8, BLOCK), f32)
@@ -538,7 +552,7 @@
             for l in range(NLIST):
                 match = tops[v][l][7:8, :] == float(b)
                 geo = geo + jnp.where(match, tops[v][l], 0.0)
-                tint = tint + jnp.where(match, pay[v, 8:16, l * BLOCK : (l + 1) * BLOCK], 0.0)
+                tint = tint + jnp.where(match, pay[v, l, 8:16, :], 0.0)
             tint_s[8 * v : 8 * v + 8, cols] = tint
         geo_out[:, cols] = geo[0:7]
     sh_out[...] = lax.dot_general(
@@ -550,7 +564,6 @@
 def body(ray_cot, ray_lists, geometry, sh_coef, view_angles, block_ids, block_counts):
     resident = geometry.shape[1]
     vmem = pl.BlockSpec(memory_space=pltpu.VMEM)
-    smem = pl.BlockSpec(memory_space=pltpu.SMEM)
     hbm = pl.BlockSpec(memory_space=pl.ANY)
 
     def room(*shape):
@@ -561,28 +574,30 @@
     payload, harmonics = pl.pallas_call(
         kernel,
         out_shape=(
-            jax.ShapeDtypeStruct((NT, 16, LIVE), f32),
+            jax.ShapeDtypeStruct((NT, NLIST, 16, BLOCK), f32),
             jax.ShapeDtypeStruct((8 * NT, 128), f32),
         ),
-        in_specs=[smem, smem, smem, vmem, vmem, hbm, hbm],
+        in_specs=[hbm, hbm, pl.BlockSpec(memory_space=pltpu.SMEM), hbm, hbm, hbm, hbm],
         out_specs=(vmem, vmem),
         scratch_shapes=[
+            room(2, NT), pltpu.VMEM((1, 1, NLIST), i32),
+            room(4, 1, RAYS), pltpu.VMEM((LISTED, RAYS), i32),
             room(7, resident), room(48, resident), room(128, RAYS),
             pltpu.VMEM((128, RAYS), i32), pltpu.VMEM((3, 32, 128), i32),
             *z_pair(2), *z_pair(8), *x_pair(8), *x_pair(16),
             *x_pair(8), *z_pair(4), *z_pair(4), *x_pair(8),
             room(10, LIVE, 128), room(LIVE, 4, 8, 128), room(LIVE, 4, 8, 128),
-            room(LIVE, 4, 8, 128), room(10, 64, 128), room(10, LIVE, 128),
-            room(128, 128), room(16, LIVE), room(NT, 16, LIVE),
+            room(LIVE, 4, 8, 128), room(10, 64, 128), room(10, 64, 128), room(LIVE, 128),
+            room(128, 128), room(NLIST, 16, BLOCK), room(NT, NLIST, 16, BLOCK),
             pltpu.SemaphoreType.DMA((4, NZ)), pltpu.SemaphoreType.DMA((4, NZ)),
             pltpu.SemaphoreType.DMA((4, PLANE)), pltpu.SemaphoreType.DMA((4, PLANE)),
-            pltpu.SemaphoreType.DMA((NT,)), pltpu.SemaphoreType.DMA((NT,)),
-            pltpu.SemaphoreType.DMA((2,)),
+            pltpu.SemaphoreType.DMA((NT, NLIST)), pltpu.SemaphoreType.DMA((NT, NLIST)),
+            pltpu.SemaphoreType.DMA((7,)),
         ],
         compiler_params=pltpu.CompilerParams(collective_id=0, has_side_effects=True),
         name="splat",
     )(
-        view_angles, block_ids[0, 0], block_counts[0], ray_cot[:, 0, :],
+        jnp.transpose(view_angles), block_ids, block_counts, ray_cot,
         jnp.transpose(ray_lists[0]), geometry, sh_coef,
     )
     return pl.pallas_call(

time: 79.5 us -> 76.5 us (0.962)
  local copies, waits for them, and re-layouts: 1.94 us -> 0 us
  Pallas kernels: 76 us -> 75.1 us
    unnamed x6 -> x0, local copies, waits for them, and re-layouts: 1.94 us -> none
    pallas_call x1, Pallas kernels: 73.8 us -> 72.9 us  [body(): pl.pallas_call(kernel, out_shape=(jax.ShapeDtypeStruct((NT, NLIST, 16, BL...]
where the time goes in v2:
time: 76.5 us; the launch traced here: 76.4 us
  Pallas kernels  75.1 us (98%)
  between operations  1.29 us (2%)
    pallas_call x1, Pallas kernels, body(): pl.pallas_call(kernel, out_shape=(jax.ShapeDtypeStruct((NT, NLIST, 16, BL...  72.9 us
    pallas_call x1, Pallas kernels, body(): pl.pallas_call(expand, out_shape=(jax.ShapeDtypeStruct((7, resident), f32...  2.19 us

profile of v2, /device:TPU:1, one launch (start us, length us, event | category | flops | bytes accessed | tf_op | source)
XLA Modules:
  0.0 76.4 jit_solution(1634645047065136407)
XLA Ops:
  1.3 72.9 %splat.1 = (f32[4,4,16,128]{3,2,1,0:T(8,128)}, f32[32,128]{1,0:T(8,128)}) custom-call(f32[2,4]{1,0:T(2,128)} %bitcast.5, s32[1,1,4]{2,1,0:T(1,128)} %ids_hbm.1, s32[1,1]{1,0:T(1,128)S(6)} %copy.9.counts, f32[4,1,256]{2,1,0:T(1,128)} %ray_cot_hbm.1, s32[8,256]{1,0:T(8,128)} %bitcast.4, f32[7,2048]{1,0:T(8,128)} %geo_hbm.1, f32[48,2048]{1,0:T(8,128)} %sh_hbm.1), custom_call_target="tpu_custom_call" | custom-call | tf_op jit(solution)/shard_map/splat/pallas_call | solution.py:574
  74.2 2.2 %expand.1 = (f32[7,2048]{1,0:T(8,128)}, f32[48,2048]{1,0:T(8,128)}) custom-call(f32[4,4,16,128]{3,2,1,0:T(8,128)} %get-tuple-element.4.pay, f32[32,128]{1,0:T(8,128)} %get-tuple-element.5.har), custom_call_target="tpu_custom_call" | custom-call | tf_op jit(solution)/shard_map/expand/pallas_call | solution.py:603
